TPU v7x, 256 devices: a whole 4x4x8 slice. The times are simulated.
256 devices in a mesh: blk: 8 (over y_hi, x), head: 8 (over z), bend: 4 (over y_lo, core).
Axes of the slice: x: 4, y: 4 (y_hi: 2, y_lo: 2; y = y_hi * 2 + y_lo), z: 8, core: 2. Of those that a mesh axis runs over, the one named last changes fastest.
Arguments:
- queries: bfloat16 [65536, 768], P(('bend', 'blk', 'head')), parts along dimension 0, may hold values from -9 to 9
- keys_values: bfloat16 [2, 65536, 768], P(None, ('bend', 'blk', 'head')), parts along dimension 1, may hold values from -6 to 6
- surface: bfloat16 [65536, 768], P(('bend', 'blk', 'head')), parts along dimension 0, may hold values from -6 to 6
- out_weight: bfloat16 [768, 768], P('head'), may hold values from -0.21875 to 0.21875
- up_weight: bfloat16 [768, 3072], P('head'), may hold values from -0.21875 to 0.21875
- down_weight: bfloat16 [3072, 768], P('head'), may hold values from -0.109375 to 0.109375
- norm_gain: float32 [768], replicated, may hold values from 0.25 to 1.75
- block_lists: int32 [256, 4], P(('bend', 'blk', 'head')), parts along dimension 0, may hold values from 0 to 63, as said below
- list_lengths: int32 [256], P(('bend', 'blk', 'head')), parts along dimension 0, may hold values from 1 to 4
Outputs:
- mixed_out: bfloat16 [65536, 768], P(('bend', 'blk', 'head')), parts along dimension 0
There are 4 independent parts, one for each index of `bend`. A program takes and returns all parts, laid end to end along the dimension named above; an argument that names none is the same for every part. Nothing has to cross between parts.
Inputs may be any that keep to these rules, and one draw needn't show every extreme that they name: `block_lists`: the list of query block b holds distinct anchor blocks, all within cycle distance 3 (modulo 64) of anchor block b, and its first entry is that block itself.
All inputs are finite; a program needn't handle non-finite values.
Results may differ from a plain program's by a relative error of at most 0.0065.
Values may be sent and summed in bfloat16 or wider, within the bound.
A program may use at most 128 MiB of HBM per device.

v0:
```python
import functools

import jax
import jax.numpy as jnp
from jax import lax
from jax.experimental import pallas as pl
from jax.experimental.pallas import tpu as pltpu
from jax.sharding import PartitionSpec as P

HEADS = 12
HD = 64
LIST = 4
REACH = 3
MESH = pl.DeviceIdType.MESH


def ring_shift(block, axis, size, distance):
    route = [(i, (i + distance) % size) for i in range(size)]
    return lax.ppermute(block, axis, route)


def x_shift(block, blk_size, x_size, distance):
    route = []
    for i in range(blk_size):
        hi, x = divmod(i, x_size)
        route.append((i, hi * x_size + (x + distance) % x_size))
    return lax.ppermute(block, "blk", route)


def core_swap(block, bend_size):
    route = [(i, i ^ 1) for i in range(bend_size)]
    return lax.ppermute(block, "bend", route)


def attention_kernel(n_blocks, mask_ref, q_ref, *refs):
    kv_refs = refs[:n_blocks]
    o_ref = refs[n_blocks]
    m_scr, l_scr, acc_scr = refs[n_blocks + 1:]
    scale = 1.0 / HD**0.5
    q_t = q_ref[...].T
    first = lax.broadcasted_iota(jnp.int32, q_t.shape, 0) < HD
    zero = jnp.zeros_like(q_t)
    halves = (jnp.where(first, q_t, zero), jnp.where(first, zero, q_t))
    for hh in range(2):
        m_scr[hh] = jnp.full(m_scr.shape[1:], -jnp.inf, jnp.float32)
        l_scr[hh] = jnp.zeros(l_scr.shape[1:], jnp.float32)
        acc_scr[hh] = jnp.zeros(acc_scr.shape[1:], jnp.float32)
    for j in range(n_blocks):
        @pl.when(mask_ref[j] > 0)
        def _():
            k = kv_refs[j][0]
            for hh in range(2):
                s_t = jnp.dot(k, halves[hh], preferred_element_type=jnp.float32) * scale
                m_scr[hh] = jnp.maximum(m_scr[hh], jnp.max(s_t, axis=0, keepdims=True))
    for j in range(n_blocks):
        @pl.when(mask_ref[j] > 0)
        def _():
            k = kv_refs[j][0]
            v_t = kv_refs[j][1].T
            for hh in range(2):
                s_t = jnp.dot(k, halves[hh], preferred_element_type=jnp.float32) * scale
                w_t = jnp.exp(s_t - m_scr[hh])
                l_scr[hh] += jnp.sum(w_t, axis=0, keepdims=True)
                acc_scr[hh] += jnp.dot(v_t, w_t.astype(jnp.bfloat16),
                                       preferred_element_type=jnp.float32)
    lane = lax.broadcasted_iota(jnp.int32, acc_scr.shape[1:], 0) < HD
    out_t = jnp.where(lane, acc_scr[0] / l_scr[0], acc_scr[1] / l_scr[1])
    o_ref[...] = out_t.T.astype(o_ref.dtype)


def attend(mask, q, blocks):
    rows, width = q.shape
    n_blocks = len(blocks)
    pair = 2 * HD
    grid_spec = pltpu.PrefetchScalarGridSpec(
        num_scalar_prefetch=1,
        grid=(width // pair,),
        in_specs=[pl.BlockSpec((rows, pair), lambda p, m: (0, p))]
        + [pl.BlockSpec((2, rows, pair), lambda p, m: (0, 0, p))] * n_blocks,
        out_specs=pl.BlockSpec((rows, pair), lambda p, m: (0, p)),
        scratch_shapes=[
            pltpu.VMEM((2, 1, rows), jnp.float32),
            pltpu.VMEM((2, 1, rows), jnp.float32),
            pltpu.VMEM((2, pair, rows), jnp.float32),
        ],
    )
    return pl.pallas_call(
        functools.partial(attention_kernel, n_blocks),
        grid_spec=grid_spec,
        out_shape=jax.ShapeDtypeStruct((rows, width), jnp.bfloat16),
        cost_estimate=pl.CostEstimate(
            flops=12 * rows * rows * width * 4,
            transcendentals=rows * rows * HEADS * 4,
            bytes_accessed=2 * rows * width * (2 * n_blocks + 2),
        ),
    )(mask, q, *blocks)


def spread_kernel(x_size, lists_ref, lengths_ref, q_ref, kv, packed,
                  ctx_ref, up_full, down_full, out_full,
                  slots, q_t, m_scr, l_scr, acc_scr, zbuf,
                  send_sems, recv_sems, local_sems, kv_send, kv_recv, z_send, z_recv):
    blk = lax.axis_index("blk")
    head = lax.axis_index("head")
    bend = lax.axis_index("bend")
    hi, x = blk // x_size, blk % x_size
    c = bend % 2
    left = (hi * x_size + (x + x_size - 1) % x_size, head, bend)
    right = (hi * x_size + (x + 1) % x_size, head, bend)
    partner = (blk, head, bend + 1 - 2 * c)
    n_head = lax.axis_size("head")
    n_ring = lax.axis_size("blk") * n_head
    me = blk * n_head + head
    ring_right = ((me + 1) % n_ring // n_head, (me + 1) % n_head, bend)
    ring_left = ((me + n_ring - 1) % n_ring // n_head, (me + n_ring - 1) % n_head, bend)
    z_right = (blk, (head + 1) % n_head, bend)
    z_left = (blk, (head + n_head - 1) % n_head, bend)
    piece_rows = packed.shape[0] // 3
    up_z = zbuf.at[:, pl.ds(piece_rows, piece_rows)]
    down_z = zbuf.at[:, pl.ds(2 * piece_rows, piece_rows)]
    out_z = zbuf.at[:, pl.ds(0, piece_rows)]
    p_own = x * 2 + c
    p_left = ((x + x_size - 1) % x_size) * 2 + c
    p_right = ((x + 1) % x_size) * 2 + c
    p_far = ((x + 2) % x_size) * 2 + c
    width = packed.shape[1]
    heads = zbuf.shape[0]
    pair = 2 * HD
    n_pairs = q_ref.shape[1] // pair
    scale = 1.0 / HD**0.5

    live = lengths_ref[0]
    biases = []
    for off in [0] + [s * dist for dist in range(1, REACH + 1) for s in (-1, 1)]:
        block_id = (me + off + n_ring) % n_ring
        listed = lists_ref[0, 0] == block_id
        for i in range(1, LIST):
            listed = listed | ((lists_ref[0, i] == block_id) & (i < live))
        biases.append(jnp.where(listed, jnp.float32(0.0), jnp.float32(-1e30)))

    barrier = pltpu.get_barrier_semaphore()
    for dev in (left, right, partner, ring_left, ring_right, z_left, z_right):
        pl.semaphore_signal(barrier, inc=1, device_id=dev, device_id_type=MESH)
    pl.semaphore_wait(barrier, 7)

    def z_send_to(src_head, k, dev, part=None):
        if part is None:
            rows_sel = slice(None)
        else:
            rows_sel = pl.ds(part * (3 * piece_rows // 2), 3 * piece_rows // 2)
        src = packed if src_head is None else zbuf.at[src_head]
        dst_head = head if src_head is None else src_head
        copy = pltpu.make_async_remote_copy(
            src_ref=src.at[rows_sel], dst_ref=zbuf.at[dst_head, rows_sel],
            send_sem=z_send.at[k], recv_sem=z_recv.at[k], device_id=dev, device_id_type=MESH)
        copy.start()
        return copy

    half_cols = q_ref.shape[1] // 2

    def kv_send_to(src, slot, dev):
        copies = []
        for part in range(2):
            cols = pl.ds(part * half_cols, half_cols)
            copy = pltpu.make_async_remote_copy(
                src_ref=src.at[:, :, cols], dst_ref=slots.at[slot, :, :, cols],
                send_sem=kv_send.at[2 * slot + part], recv_sem=kv_recv.at[2 * slot + part],
                device_id=dev, device_id_type=MESH)
            copy.start()
            copies.append(copy)
        return copies

    def up_at(p, part=None):
        cols = pl.ds(pl.multiple_of((p // 2) * width, 128), width)
        if part is None:
            return up_full.at[:, c, :, cols]
        return up_full.at[pl.ds(part * (heads // 2), heads // 2), c, :, cols]

    def down_at(p, part=None):
        if part is None:
            return down_full.at[:, p]
        return down_full.at[pl.ds(part * (heads // 2), heads // 2), p]

    def send(src, dst, k, dev):
        copy = pltpu.make_async_remote_copy(
            src_ref=src, dst_ref=dst, send_sem=send_sems.at[k], recv_sem=recv_sems.at[k],
            device_id=dev, device_id_type=MESH)
        copy.start()
        return copy

    kv_sent = [kv_send_to(kv, 0, ring_right), kv_send_to(kv, 1, ring_left)]
    own_z = pltpu.make_async_copy(packed, zbuf.at[head], local_sems.at[3])
    own_z.start()
    z_sent = [z_send_to(None, 0, z_right), z_send_to(None, 1, z_left)]

    first = lax.broadcasted_iota(jnp.int32, (pair, q_ref.shape[0]), 0) < HD
    for p in range(n_pairs):
        qp = q_ref[:, p * pair:(p + 1) * pair].T
        q_t[2 * p] = jnp.where(first, qp, jnp.zeros_like(qp))
        q_t[2 * p + 1] = jnp.where(first, jnp.zeros_like(qp), qp)
    m_scr[...] = jnp.full(m_scr.shape, -jnp.inf, jnp.float32)
    l_scr[...] = jnp.zeros(l_scr.shape, jnp.float32)
    acc_scr[...] = jnp.zeros(acc_scr.shape, jnp.float32)

    def absorb(block, bias, lo=0, hi_pair=None):
        def one_pair(p, carry):
            cols = pl.ds(pl.multiple_of(p * pair, pair), pair)
            k = block[0, :, cols]
            v_t = block[1, :, cols].T
            for hh in range(2):
                h = 2 * p + hh
                s_t = jnp.dot(k, q_t[h], preferred_element_type=jnp.float32) * scale + bias
                m_old = m_scr[h]
                m_new = jnp.maximum(m_old, jnp.max(s_t, axis=0, keepdims=True))
                alpha = jnp.exp(m_old - m_new)
                w_t = jnp.exp(s_t - m_new)
                l_scr[h] = alpha * l_scr[h] + jnp.sum(w_t, axis=0, keepdims=True)
                acc_scr[h] = alpha * acc_scr[h] + jnp.dot(
                    v_t, w_t.astype(jnp.bfloat16), preferred_element_type=jnp.float32)
                m_scr[h] = m_new
            return carry
        lax.fori_loop(lo, n_pairs if hi_pair is None else hi_pair, one_pair, 0)

    def wait_kv(slot, part):
        kv_sent[slot][part].wait_recv()

    absorb(kv, biases[0])

    for dist in range(1, n_head // 2):
        z_sent[2 * dist - 2].wait_recv()
        z_sent[2 * dist - 1].wait_recv()
        from_left = (head + n_head - dist) % n_head
        from_right = (head + dist) % n_head
        if dist < n_head // 2 - 1:
            z_sent += [z_send_to(from_left, 2 * dist, z_right),
                       z_send_to(from_right, 2 * dist + 1, z_left)]
        else:
            z_sent += [z_send_to(from_left, 2 * dist, z_right, 0),
                       z_send_to(from_right, 2 * dist + 1, z_left, 1)]
        if dist == 1:
            for slot in (0, 1):
                wait_kv(slot, 0)
                wait_kv(slot, 1)
            kv_sent += [kv_send_to(slots.at[0], 2, ring_right),
                        kv_send_to(slots.at[1], 3, ring_left)]
    z_sent[-2].wait_recv()
    z_sent[-1].wait_recv()
    own_z.wait()

    local = [
        pltpu.make_async_copy(up_z, up_at(p_own), local_sems.at[0]),
        pltpu.make_async_copy(down_z, down_at(p_own), local_sems.at[1]),
        pltpu.make_async_copy(out_z, out_full.at[:, c], local_sems.at[2]),
    ]
    for copy in local:
        copy.start()
    a_up_r = send(up_z, up_at(p_own), 0, right)
    a_up_l = send(up_z, up_at(p_own), 1, left)
    a_dn_r = send(down_z, down_at(p_own), 2, right)
    a_dn_l = send(down_z, down_at(p_own), 3, left)
    sent = [a_up_r, a_up_l, a_dn_r, a_dn_l]
    sent += [
        send(out_z, out_full.at[:, c], 4, partner),
        send(up_z, up_at(p_own), 5, partner),
        send(down_z, down_at(p_own), 6, partner),
    ]
    a_up_r.wait_recv()
    a_dn_r.wait_recv()
    b_up_r = send(up_at(p_left, 0), up_at(p_left, 0), 7, right)
    b_dn_r = send(down_at(p_left, 0), down_at(p_left, 0), 8, right)
    sent += [b_up_r, b_dn_r]
    sent += [send(up_at(p_left), up_at(p_left), 9, partner),
             send(down_at(p_left), down_at(p_left), 10, partner)]
    a_up_l.wait_recv()
    a_dn_l.wait_recv()
    b_up_l = send(up_at(p_right, 1), up_at(p_right, 1), 11, left)
    b_dn_l = send(down_at(p_right, 1), down_at(p_right, 1), 12, left)
    sent += [b_up_l, b_dn_l]
    sent += [send(up_at(p_right), up_at(p_right), 13, partner),
             send(down_at(p_right), down_at(p_right), 14, partner)]

    for slot in (2, 3):
        wait_kv(slot, 0)
        wait_kv(slot, 1)
    kv_sent += [kv_send_to(slots.at[2], 4, ring_right), kv_send_to(slots.at[3], 5, ring_left)]

    b_up_r.wait_recv()
    b_dn_r.wait_recv()
    sent += [send(up_at(p_far, 0), up_at(p_far, 0), 15, partner),
             send(down_at(p_far, 0), down_at(p_far, 0), 16, partner)]
    b_up_l.wait_recv()
    b_dn_l.wait_recv()
    sent += [send(up_at(p_far, 1), up_at(p_far, 1), 17, partner),
             send(down_at(p_far, 1), down_at(p_far, 1), 18, partner)]

    absorb(slots.at[0], biases[1])
    absorb(slots.at[1], biases[2])
    absorb(slots.at[2], biases[3])
    absorb(slots.at[3], biases[4])

    half_pairs = n_pairs // 2
    wait_kv(4, 0)
    absorb(slots.at[4], biases[5], 0, half_pairs)
    wait_kv(5, 0)
    absorb(slots.at[5], biases[6], 0, half_pairs)
    wait_kv(4, 1)
    absorb(slots.at[4], biases[5], half_pairs, n_pairs)
    wait_kv(5, 1)
    absorb(slots.at[5], biases[6], half_pairs, n_pairs)

    row = lax.broadcasted_iota(jnp.int32, (pair, q_ref.shape[0]), 0) < HD

    def write_pair(p, carry):
        out_t = jnp.where(row, acc_scr[2 * p] / l_scr[2 * p], acc_scr[2 * p + 1] / l_scr[2 * p + 1])
        ctx_ref[:, pl.ds(pl.multiple_of(p * pair, pair), pair)] = out_t.T.astype(ctx_ref.dtype)
        return carry
    lax.fori_loop(0, n_pairs, write_pair, 0)

    for k in (4, 5, 6, 9, 10, 13, 14, 15, 16, 17, 18):
        sent[k].wait_recv()
    for copy in sent + [c for pair_ in kv_sent for c in pair_] + z_sent:
        copy.wait_send()
    for copy in local:
        copy.wait()


def exchange(lists, lengths, q, kv, packed, n_heads, x_size):
    piece_rows, d = packed.shape[0] // 3, packed.shape[1]
    n_rows = q.shape[0]
    n_pieces = 2 * x_size
    any_spec = pl.BlockSpec(memory_space=pl.ANY)
    vmem_spec = pl.BlockSpec(memory_space=pltpu.VMEM)
    return pl.pallas_call(
        functools.partial(spread_kernel, x_size),
        out_shape=(
            jax.ShapeDtypeStruct(q.shape, jnp.bfloat16),
            jax.ShapeDtypeStruct((n_heads, 2, piece_rows, x_size * d), packed.dtype),
            jax.ShapeDtypeStruct((n_heads, n_pieces, piece_rows, d), packed.dtype),
            jax.ShapeDtypeStruct((n_heads, 2, piece_rows, d), packed.dtype),
        ),
        in_specs=[pl.BlockSpec(memory_space=pltpu.SMEM)] * 2 + [vmem_spec] * 3,
        out_specs=(vmem_spec, any_spec, any_spec, any_spec),
        scratch_shapes=[
            pltpu.VMEM((2 * REACH,) + kv.shape, kv.dtype),
            pltpu.VMEM((HEADS, 2 * HD, n_rows), jnp.bfloat16),
            pltpu.VMEM((HEADS, 1, n_rows), jnp.float32),
            pltpu.VMEM((HEADS, 1, n_rows), jnp.float32),
            pltpu.VMEM((HEADS, 2 * HD, n_rows), jnp.float32),
            pltpu.VMEM((n_heads,) + packed.shape, packed.dtype),
            pltpu.SemaphoreType.DMA((19,)),
            pltpu.SemaphoreType.DMA((19,)),
            pltpu.SemaphoreType.DMA((4,)),
            pltpu.SemaphoreType.DMA((4 * REACH,)),
            pltpu.SemaphoreType.DMA((4 * REACH,)),
            pltpu.SemaphoreType.DMA((n_heads,)),
            pltpu.SemaphoreType.DMA((n_heads,)),
        ],
        compiler_params=pltpu.CompilerParams(
            collective_id=1, has_side_effects=True, vmem_limit_bytes=48 * 1024 * 1024),
        cost_estimate=pl.CostEstimate(
            flops=6 * n_rows * n_rows * q.shape[1] * (2 * REACH + 1),
            transcendentals=n_rows * n_rows * HEADS * (2 * REACH + 1),
            bytes_accessed=2 * n_heads * piece_rows * d * (3 * n_pieces),
        ),
    )(lists, lengths, q, kv, packed)


def shards(
    queries,
    keys_values,
    surface,
    out_weight,
    up_weight,
    down_weight,
    norm_gain,
    block_lists,
    list_lengths,
):
    row_count, feature_width = queries.shape
    loop_size = lax.axis_size(("blk", "head"))
    blk_size = lax.axis_size("blk")
    bend_size = lax.axis_size("bend")
    x_size = 4
    own_index = lax.axis_index(("blk", "head"))
    x = lax.axis_index("blk") % x_size
    core = lax.axis_index("bend") % 2
    piece = x * 2 + core
    n_pieces = 2 * x_size

    head_size = lax.axis_size("head")
    d = feature_width
    out_rows = out_weight.shape[0] // 2
    down_rows = down_weight.shape[0] // n_pieces
    up_rows = up_weight.shape[0] // 2
    packed = jnp.concatenate([
        lax.dynamic_slice_in_dim(out_weight, core * out_rows, out_rows, axis=0),
        lax.dynamic_slice(up_weight, (core * up_rows, x * d), (up_rows, d)),
        lax.dynamic_slice_in_dim(down_weight, piece * down_rows, down_rows, axis=0),
    ], axis=0)
    context, up_full, down_full, out_full = exchange(
        block_lists, list_lengths, queries, keys_values, packed, head_size, x_size)
    out_full = out_full.reshape(d, d)
    up_full = up_full.reshape(d, -1)
    down_full = down_full.reshape(-1, d)

    hidden = surface.astype(jnp.float32) + jnp.dot(
        context, out_full, preferred_element_type=jnp.float32)
    mean_square = jnp.mean(hidden * hidden, axis=1, keepdims=True)
    normed = (hidden * lax.rsqrt(mean_square + 1e-05) * norm_gain[None, :]).astype(jnp.bfloat16)
    pre_gelu = jnp.dot(normed, up_full, preferred_element_type=jnp.float32)
    activated = jax.nn.gelu(pre_gelu, approximate=True).astype(jnp.bfloat16)
    mixed_out = hidden + jnp.dot(activated, down_full, preferred_element_type=jnp.float32)
    return mixed_out.astype(jnp.bfloat16)


def solution(mesh):
    return jax.shard_map(
        shards,
        mesh=mesh,
        in_specs=(
            P(("bend", "blk", "head"), None),
            P(None, ("bend", "blk", "head"), None),
            P(("bend", "blk", "head"), None),
            P("head", None),
            P("head", None),
            P("head", None),
            P(),
            P(("bend", "blk", "head"), None),
            P(("bend", "blk", "head")),
        ),
        out_specs=P(("bend", "blk", "head"), None),
        check_vma=False,
    )
```

profile of v0, /device:TPU:8, one launch (start us, length us, event | category | flops | bytes accessed | tf_op | source)
XLA Modules:
  0.0 163.4 jit_solution(1881440634331187316)
XLA Ops:
  0.7 0.9 dynamic_slice.10
  1.5 0.9 constant_dynamic-slice_fusion
  2.5 0.0 copy-start
  2.5 1.1 copy-done
  3.6 0.0 copy-start.1
  3.6 1.0 copy-done.1
  4.6 0.0 copy-start.2
  4.6 0.7 copy-done.2
  5.3 0.0 copy-start.3
  5.3 0.0 copy-start.4
  5.3 150.0 %shard_map.91 = (bf16[256,768]{1,0:T(8,128)(2,1)S(1)}, bf16[8,2,48,3072]{3,2,1,0:T(8,128)(2,1)}, bf16[8,8,48,768]{3,2,1,0:T(8,128)(2,1)}, bf16[8,2,48,768]{3,2,1,0:T(8,128)(2,1)S(1)}) custom-call(s32[1,4]{1,0:T(1,128)S(1)} %copy-done.2, s32[1]{0:T(128)S(6)} %copy.10.lengths_ref, bf16[256,768]{1,0:T(8,128)(2,1)S(1)} %copy-done.1, ...), custom_call_target="tpu_custom_call" | custom-call | flops 2113929216 | bytes 14155776 | tf_op jit(solution)/shard_map/pallas_call | solution.py:333
  155.3 0.0 copy-done.3
  155.3 0.6 multiply_reduce_fusion
  155.9 0.0 copy-done.4
  155.9 7.5 %fusion.17 = bf16[256,768]{1,0:T(8,128)(2,1)} fusion(f32[256,768]{1,0:T(8,128)S(1)} %get-tuple-element.14, bf16[3072,768]{1,0:T(8,128)(2,1)} %bitcast.9, bf16[768,3072]{1,0:T(8,128)(2,1)} %bitcast.8, f32[768]{0:T(1024)S(1)} %copy-done.4, f32[256]{0:T(256)S(1)} %add_rsqrt_fusion), kind=kOutput, calls=%fused_computation.16 | convolution fusion | flops 2423980032 | bytes 10620928 | tf_op jit(solution)/shard_map/dot_general | solution.py:412
  (2 shorter events, 0.0 us)
Async XLA Ops:
  2.5 1.1 copy-start
  3.6 1.0 copy-start.1
  4.6 0.7 copy-start.2
  5.3 150.0 %copy-start.3 = (bf16[256,768]{1,0:T(8,128)(2,1)S(1)}, bf16[256,768]{1,0:T(8,128)(2,1)}, u32[]{:S(2)}) copy-start(bf16[256,768]{1,0:T(8,128)(2,1)} %param.11) | copy-start | bytes 1179652
  5.3 150.6 %copy-start.4 = (f32[768]{0:T(1024)S(1)}, f32[768]{0:T(1024)}, u32[]{:S(2)}) copy-start(f32[768]{0:T(1024)} %param.15) | copy-start | bytes 9220
where the time goes:
time: 164 us; the launch traced here: 163 us
  Pallas kernels  150 us (91%)
  matrix products  8.09 us (5%)
  local copies, waits for them, and re-layouts  4.61 us (3%)
    pallas_call x1, Pallas kernels, exchange(): pl.pallas_call(functools.partial(spread_kernel, x_size), out_shape=(jax.S...  150 us
    dot_general x1, matrix products, shards(): jnp.dot(activated, down_full, preferred_element_type=jnp.float32)  7.53 us

commit v1 on v0

--- a/solution.py
+++ b/solution.py
@@ -243,6 +243,8 @@
                 wait_kv(slot, 1)
             kv_sent += [kv_send_to(slots.at[0], 2, ring_right),
                         kv_send_to(slots.at[1], 3, ring_left)]
+            absorb(slots.at[0], biases[1])
+            absorb(slots.at[1], biases[2])
     z_sent[-2].wait_recv()
     z_sent[-1].wait_recv()
     own_z.wait()
@@ -279,11 +281,11 @@
     sent += [send(up_at(p_right), up_at(p_right), 13, partner),
              send(down_at(p_right), down_at(p_right), 14, partner)]
 
+
     for slot in (2, 3):
         wait_kv(slot, 0)
         wait_kv(slot, 1)
     kv_sent += [kv_send_to(slots.at[2], 4, ring_right), kv_send_to(slots.at[3], 5, ring_left)]
-
     b_up_r.wait_recv()
     b_dn_r.wait_recv()
     sent += [send(up_at(p_far, 0), up_at(p_far, 0), 15, partner),
@@ -293,8 +295,6 @@
     sent += [send(up_at(p_far, 1), up_at(p_far, 1), 17, partner),
              send(down_at(p_far, 1), down_at(p_far, 1), 18, partner)]
 
-    absorb(slots.at[0], biases[1])
-    absorb(slots.at[1], biases[2])
     absorb(slots.at[2], biases[3])
     absorb(slots.at[3], biases[4])
 

time: 164 us -> 155 us (0.945)
  Pallas kernels: 150 us -> 142 us
    pallas_call x1, Pallas kernels: 150 us -> 142 us  [exchange(): pl.pallas_call(functools.partial(spread_kernel, x_size), out_shape=(jax.S...]
where the time goes in v1:
time: 155 us
  Pallas kernels  142 us (92%)
  matrix products  8.09 us (5%)
  local copies, waits for them, and re-layouts  4.61 us (3%)
    pallas_call x1, Pallas kernels, exchange(): pl.pallas_call(functools.partial(spread_kernel, x_size), out_shape=(jax.S...  142 us
    dot_general x1, matrix products, shards(): jnp.dot(activated, down_full, preferred_element_type=jnp.float32)  7.53 us

profile of v1, /device:TPU:8, one launch (start us, length us, event | category | flops | bytes accessed | tf_op | source)
XLA Modules:
  0.0 155.2 jit_solution(6111295617616144)
XLA Ops:
  0.7 0.9 dynamic_slice.10
  1.5 0.9 constant_dynamic-slice_fusion
  2.5 0.0 copy-start
  2.5 1.1 copy-done
  3.6 0.0 copy-start.1
  3.6 1.0 copy-done.1
  4.6 0.0 copy-start.2
  4.6 0.7 copy-done.2
  5.3 0.0 copy-start.3
  5.3 0.0 copy-start.4
  5.3 141.7 %shard_map.91 = (bf16[256,768]{1,0:T(8,128)(2,1)S(1)}, bf16[8,2,48,3072]{3,2,1,0:T(8,128)(2,1)}, bf16[8,8,48,768]{3,2,1,0:T(8,128)(2,1)}, bf16[8,2,48,768]{3,2,1,0:T(8,128)(2,1)S(1)}) custom-call(s32[1,4]{1,0:T(1,128)S(1)} %copy-done.2, s32[1]{0:T(128)S(6)} %copy.10.lengths_ref, bf16[256,768]{1,0:T(8,128)(2,1)S(1)} %copy-done.1, ...), custom_call_target="tpu_custom_call" | custom-call | flops 2113929216 | bytes 14155776 | tf_op jit(solution)/shard_map/pallas_call | solution.py:333
  147.0 0.0 copy-done.3
  147.0 0.6 multiply_reduce_fusion
  147.6 0.0 copy-done.4
  147.6 7.5 %fusion.17 = bf16[256,768]{1,0:T(8,128)(2,1)} fusion(f32[256,768]{1,0:T(8,128)S(1)} %get-tuple-element.14, bf16[3072,768]{1,0:T(8,128)(2,1)} %bitcast.9, bf16[768,3072]{1,0:T(8,128)(2,1)} %bitcast.8, f32[768]{0:T(1024)S(1)} %copy-done.4, f32[256]{0:T(256)S(1)} %add_rsqrt_fusion), kind=kOutput, calls=%fused_computation.16 | convolution fusion | flops 2423980032 | bytes 10620928 | tf_op jit(solution)/shard_map/dot_general | solution.py:412
  (2 shorter events, 0.0 us)
Async XLA Ops:
  2.5 1.1 copy-start
  3.6 1.0 copy-start.1
  4.6 0.7 copy-start.2
  5.3 141.7 %copy-start.3 = (bf16[256,768]{1,0:T(8,128)(2,1)S(1)}, bf16[256,768]{1,0:T(8,128)(2,1)}, u32[]{:S(2)}) copy-start(bf16[256,768]{1,0:T(8,128)(2,1)} %param.11) | copy-start | bytes 1179652
  5.3 142.3 %copy-start.4 = (f32[768]{0:T(1024)S(1)}, f32[768]{0:T(1024)}, u32[]{:S(2)}) copy-start(f32[768]{0:T(1024)} %param.15) | copy-start | bytes 9220
